TPU v7x, 256 devices: a whole 4x4x8 slice. The times are simulated.
256 devices in a mesh: ep: 32 (over x, z), tp: 8 (over y, core).
Axes of the slice: x: 4, y: 4, z: 8, core: 2. Of those that a mesh axis runs over, the one named last changes fastest.
Arguments:
- attn_out: bfloat16 [8192, 2048], P('ep', 'tp'), may hold values from -6 to 6
- out_proj: bfloat16 [2048, 2048], P('tp'), may hold values from -0.125 to 0.125
- residual: bfloat16 [8192, 2048], P('ep'), may hold values from -40 to 40
- norm_gain: float32 [2048], replicated, may hold values from 0.25 to 1.75
- router: bfloat16 [2048, 64], replicated, may hold values from -0.125 to 0.125
- expert_gate_up: bfloat16 [256, 2, 352, 2048], P(('ep', 'tp')), may hold values from -0.125 to 0.125
- expert_down: bfloat16 [256, 352, 2048], P(('ep', 'tp')), may hold values from -0.15625 to 0.15625
- shared_gate_up: bfloat16 [2, 2816, 2048], P(None, 'tp'), may hold values from -0.125 to 0.125
- shared_down: bfloat16 [2816, 2048], P('tp'), may hold values from -0.109375 to 0.109375
- routes: int32 [8192, 6], P('ep'), may hold values from 0 to 63, all different within a row; in each aligned block of 256 rows (0 to 255, 256 to 511, ...) at most 40 rows name the same one
- live_rows: int32 [32], P('ep'), may hold values from 128 to 256, as said below
- next_gain: float32 [2048], replicated, may hold values from 0.25 to 1.75
Outputs:
- next_stream: bfloat16 [8192, 2048], P('ep', 'tp')
- next_normed: bfloat16 [8192, 2048], P('ep', 'tp')
Inputs may be any that keep to these rules, and one draw needn't show every extreme that they name: `routes`: each row names 6 different experts. Among the 256 rows of one block no expert is named by more than 40 rows, a bound that some block reaches. The live rows of block b are its first live_rows[b] rows; in every draw some block is entirely live.
All inputs are finite; a program needn't handle non-finite values.
Results may differ from a plain program's by a relative error of at most 0.012.
Values may be sent and summed in bfloat16 or wider, within the bound.
A program may use at most 128 MiB of HBM per device.

v0:
```python
import jax
import jax.numpy as jnp
from jax import lax
from jax.sharding import PartitionSpec as P

EXP_DEV = 2
norm_epsilon = 1e-06
routed_scale = 2.446


def slot_table(route_block, live_count, experts, capacity):
    fanout = route_block.shape[1]
    flat_ids = route_block.reshape(-1)
    entry_index = jnp.arange(flat_ids.shape[0], dtype=jnp.int32)
    living = entry_index // fanout < live_count
    one_hot = (
        (flat_ids[:, None] == jnp.arange(experts, dtype=jnp.int32)[None, :]) & living[:, None]
    ).astype(jnp.int32)
    earlier = jnp.cumsum(one_hot, axis=0, dtype=jnp.int32) - one_hot
    position = jnp.sum(earlier * one_hot, axis=1, dtype=jnp.int32)
    slot_index = jnp.where(living, flat_ids * capacity + position, experts * capacity)
    slot_owner = (
        jnp.full((experts * capacity,), -1, jnp.int32).at[slot_index].set(entry_index, mode="drop")
    )
    return (slot_index, living, slot_owner)


def gate_weights(normed, router, route_block):
    logits = jnp.dot(normed, router, preferred_element_type=jnp.float32)
    chosen = jnp.take_along_axis(logits, route_block, axis=1)
    scores = jax.nn.sigmoid(chosen)
    return scores / jnp.sum(scores, axis=1, keepdims=True) * routed_scale


def on_device(
    attn_out,
    out_proj,
    residual,
    norm_gain,
    router,
    expert_gate_up,
    expert_down,
    shared_gate_up,
    shared_down,
    routes,
    live_rows,
    next_gain,
):
    partial_out = jnp.dot(attn_out, out_proj, preferred_element_type=jnp.float32)
    summed = lax.psum(partial_out, "tp")
    stream = (summed + residual.astype(jnp.float32)).astype(jnp.bfloat16)
    stream_wide = stream.astype(jnp.float32)
    normed = (
        stream_wide
        * lax.rsqrt(jnp.mean(stream_wide * stream_wide, axis=1, keepdims=True) + norm_epsilon)
        * norm_gain
    ).astype(jnp.bfloat16)
    width = normed.shape[1]
    tp_count = lax.axis_size("tp")
    ep_count = lax.axis_size("ep")
    width_slice = width // tp_count
    column_start = lax.axis_index("tp") * width_slice
    unit_blocks = tp_count // EXP_DEV
    group = lax.axis_index("tp") // unit_blocks
    experts = router.shape[1]
    fanout = routes.shape[1]
    token_rows = routes.shape[0]
    capacity = token_rows * fanout * 5 // (3 * experts)
    slot_index, living, slot_owner = slot_table(routes, live_rows[0], experts, capacity)
    owners = slot_owner.reshape(ep_count, EXP_DEV, capacity)
    filled = owners >= 0
    source_row = jnp.where(filled, owners // fanout, 0)
    dispatched = jnp.where(filled[:, :, :, None], normed[source_row], jnp.zeros((), jnp.bfloat16))
    rows = lax.dynamic_index_in_dim(
        lax.all_to_all(dispatched, "ep", split_axis=0, concat_axis=0, tiled=True),
        group,
        1,
        keepdims=False,
    )
    gate_proj = jnp.einsum(
        "scd,fd->scf", rows, expert_gate_up[0, 0], preferred_element_type=jnp.float32
    )
    up_proj = jnp.einsum(
        "scd,fd->scf", rows, expert_gate_up[0, 1], preferred_element_type=jnp.float32
    )
    hidden = (jax.nn.silu(gate_proj) * up_proj).astype(jnp.bfloat16)
    produced = jnp.einsum(
        "scf,fd->scd", hidden, expert_down[0], preferred_element_type=jnp.float32
    ).astype(jnp.bfloat16)
    returned = lax.all_to_all(produced, "ep", split_axis=0, concat_axis=0, tiled=True)
    flat_terms = returned.reshape(ep_count * capacity, width)
    living_pairs = living.reshape(token_rows, fanout)
    mine = living_pairs & (routes % EXP_DEV == group)
    position = slot_index.reshape(token_rows, fanout) - routes * capacity
    term_row = jnp.where(mine, routes // EXP_DEV * capacity + position, 0)
    weights = gate_weights(normed, router, routes) * mine.astype(jnp.float32)
    picked = flat_terms[term_row]
    routed_part = jnp.einsum("tkd,tk->td", picked.astype(jnp.float32), weights)
    shared_gate = jnp.einsum(
        "td,fd->tf", normed, shared_gate_up[0], preferred_element_type=jnp.float32
    )
    shared_up = jnp.einsum(
        "td,fd->tf", normed, shared_gate_up[1], preferred_element_type=jnp.float32
    )
    shared_hidden = (jax.nn.silu(shared_gate) * shared_up).astype(jnp.bfloat16)
    shared_part = jnp.dot(shared_hidden, shared_down, preferred_element_type=jnp.float32)
    combined = lax.psum_scatter(
        (routed_part + shared_part).astype(jnp.bfloat16), "tp", scatter_dimension=1, tiled=True
    ).astype(jnp.float32)
    stream_slice = lax.dynamic_slice_in_dim(stream, column_start, width_slice, 1)
    next_stream = (stream_slice.astype(jnp.float32) + combined).astype(jnp.bfloat16)
    next_wide = next_stream.astype(jnp.float32)
    squares = lax.psum(jnp.sum(next_wide * next_wide, axis=1), "tp")
    gain_slice = lax.dynamic_slice_in_dim(next_gain, column_start, width_slice, 0)
    next_normed = (
        next_wide * lax.rsqrt(squares[:, None] / width + norm_epsilon) * gain_slice
    ).astype(jnp.bfloat16)
    return (next_stream, next_normed)


def solution(mesh):
    in_specs = (
        P("ep", "tp"),
        P("tp", None),
        P("ep", None),
        P(),
        P(),
        P(("ep", "tp"), None, None, None),
        P(("ep", "tp"), None, None),
        P(None, "tp", None),
        P("tp", None),
        P("ep", None),
        P("ep"),
        P(),
    )
    out_specs = (P("ep", "tp"), P("ep", "tp"))
    return jax.shard_map(
        on_device, mesh=mesh, in_specs=in_specs, out_specs=out_specs, check_vma=False
    )
```

profile of v0, /device:TPU:1, one launch (start us, length us, event | category | flops | bytes accessed | tf_op | source)
XLA Modules:
  0.0 608.2 jit_solution(8504731297024068242)
XLA Ops:
  7.2 0.0 copy-start
  7.2 0.0 copy-start.4
  7.2 0.0 all-reduce.2.cloned.1.call-start
  7.2 3.1 fusion.76
  10.4 0.0 all-reduce.2.cloned.1.call-update
  10.4 0.0 copy-done.4
  10.4 0.1 copy.42
  10.5 0.1 eq.37
  10.7 0.1 eq.33
  11.5 0.1 fusion.37
  11.6 18.1 %reduce-window.6 = s32[64,12,128]{2,1,0:T(8,128)S(1)} reduce-window(s32[64,12,128]{2,1,0:T(8,128)S(1)} %fusion.37, s32[]{:T(128)} %constant.103.clone.1), window={size=1x1x128 pad=0_0x0_0x127_0}, to_apply=%region_1.0 | reduce-window | flops 12484608 | bytes 786436 | tf_op jit(solution)/shard_map/reduce-window
  29.7 0.2 slice.30
  29.9 0.3 copy.44
  30.2 0.1 copy.45
  30.3 0.2 broadcast_add_fusion
  30.5 0.2 fusion.40
  30.7 0.1 reduce_sum.43
  30.9 0.1 copy.46
  31.0 0.1 copy.41
  31.1 0.1 mul.91
  31.3 6.2 %scatter_custom_fusion = s32[2560]{0:T(1024)S(1)} fusion(s32[1536]{0:T(1024)S(1)} %fusion.67, s32[1536]{0:T(1024)S(1)} %iota.72, s32[]{:T(128)} %constant.107.clone.1), kind=kCustom, calls=%fused_computation.112 | custom fusion | bytes 10244 | tf_op jit(solution)/shard_map/scatter | solution.py:23
  37.5 0.1 ge.28
  37.7 0.7 ge.27
  38.4 0.1 div.89
  38.5 0.1 and.83
  38.6 0.1 compare_select_fusion
  38.7 0.1 reshape.223
  38.8 0.6 pad_clamp_fusion
  39.4 44.1 %all-reduce.2.cloned.1.call-done = f32[256,2048]{1,0:T(8,128)} async-done(((f32[256,2048]{1,0:T(8,128)}), f32[256,2048]{1,0:T(8,128)}) %all-reduce.2.cloned.1.call-update) | async-done | bytes 2097168 | tf_op jit(solution)/shard_map/psum | solution.py:50
  83.4 2.3 fusion.7
  85.7 0.0 copy-done.5
  85.7 0.3 fusion.9
  86.0 10.9 %gather_fusion = bf16[2560,2048]{1,0:T(8,128)(2,1)} fusion(bf16[256,2048]{1,0:T(8,128)(2,1)S(1)} %fusion.9, s32[3072]{0:T(1024)} %pad_clamp_fusion), kind=kCustom, calls=%fused_computation | custom fusion | bytes 20981760 | tf_op jit(solution)/shard_map/gather | solution.py:73
  97.0 10.0 %broadcast_select_fusion = bf16[32,2,40,2048]{3,2,1,0:T(8,128)(2,1)} fusion(bf16[32,2,40,2048]{3,2,1,0:T(8,128)(2,1)} %bitcast.83, pred[32,2,40]{2,1,0:T(4,128)(4,1)} %ge.27), kind=kLoop, calls=%fused_computation.4 | loop fusion | flops 5242880 | bytes 20974080 | tf_op jit(solution)/shard_map/jit(_where)/select_n | solution.py:73
  106.9 9.7 %all-to-all-start = ((bf16[32,2,40,2048]{3,2,1,0:T(8,128)(2,1)}), bf16[32,2,40,2048]{3,2,1,0:T(8,128)(2,1)}, u32[]{:S(2)}, u32[]{:S(2)}) async-start(bf16[32,2,40,2048]{3,2,1,0:T(8,128)(2,1)} %broadcast_select_fusion), calls=%async_computation | async-start | bytes 20971520 | tf_op jit(solution)/shard_map/all_to_all | solution.py:75
  116.6 232.0 %all-to-all-done = bf16[32,2,40,2048]{3,2,1,0:T(8,128)(2,1)} async-done(((bf16[32,2,40,2048]{3,2,1,0:T(8,128)(2,1)}), bf16[32,2,40,2048]{3,2,1,0:T(8,128)(2,1)}, u32[]{:S(2)}, u32[]{:S(2)}) %all-to-all-start) | async-done | bytes 10485792 | tf_op jit(solution)/shard_map/all_to_all | solution.py:75
  348.6 7.1 %fusion.2 = f32[32,40,352]{2,1,0:T(8,128)} fusion(bf16[32,2,40,2048]{3,2,1,0:T(8,128)(2,1)} %all-to-all-done, s32[]{:T(128)S(6)} %select_n.135, bf16[1,2,352,2048]{3,2,1,0:T(8,128)(2,1)} %param.17), kind=kOutput, calls=%fused_computation.7 | convolution fusion | flops 1845493760 | bytes 8486916 | tf_op jit(solution)/shard_map/scd,fd->scf/dot_general | solution.py:80
  355.7 0.0 copy-done
  355.7 9.8 %convolution_convert_fusion = bf16[32,40,2048]{2,1,0:T(8,128)(2,1)} fusion(bf16[1,352,2048]{2,1,0:T(8,128)(2,1)S(1)} %copy-done, f32[32,40,352]{2,1,0:T(8,128)} %fusion.2, bf16[32,2,40,2048]{3,2,1,0:T(8,128)(2,1)} %all-to-all-done, s32[]{:T(128)S(6)} %select_n.135, bf16[1,2,352,2048]{3,2,1,0:T(8,128)(2,1)} %param.17), kind=kOutput, calls=%fused_computation.11 | convolution fusion | flops 3696312320 | bytes 15335428 | tf_op jit(solution)/shard_map/scf,fd->scd/dot_general | solution.py:87
  365.5 10.2 %all-to-all-start.1 = ((bf16[32,40,2048]{2,1,0:T(8,128)(2,1)}), bf16[32,40,2048]{2,1,0:T(8,128)(2,1)}, u32[]{:S(2)}, u32[]{:S(2)}) async-start(bf16[32,40,2048]{2,1,0:T(8,128)(2,1)} %convolution_convert_fusion), calls=%async_computation.1 | async-start | bytes 10485760 | tf_op jit(solution)/shard_map/all_to_all | solution.py:90
  375.7 0.2 reduce-scatter.2.cloned.1.call-start
  375.9 0.1 copy.47
  376.1 0.1 reshape.231
  376.2 0.1 copy.48
  376.4 0.1 reshape.237
  376.6 0.0 copy-done.3
  376.6 0.4 fusion.77
  377.0 12.7 %gather_fusion.2 = f32[1536]{0:T(1024)S(1)} fusion(f32[256,64]{0,1:T(8,128)S(1)} %fusion.77, s32[1536]{0:T(1024)S(1)} %reshape.237), kind=kCustom, calls=%fused_computation.2 | custom fusion | bytes 24576 | tf_op jit(solution)/shard_map/jit(take_along_axis)/gather | solution.py:30
  389.7 0.1 reshape.240
  389.9 0.1 copy.49
  390.0 0.2 copy.50
  390.2 2.7 fusion.16
  392.9 99.9 %all-to-all-done.1 = bf16[32,40,2048]{2,1,0:T(8,128)(2,1)} async-done(((bf16[32,40,2048]{2,1,0:T(8,128)(2,1)}), bf16[32,40,2048]{2,1,0:T(8,128)(2,1)}, u32[]{:S(2)}, u32[]{:S(2)}) %all-to-all-start.1) | async-done | bytes 5242912 | tf_op jit(solution)/shard_map/all_to_all | solution.py:90
  492.8 15.8 %gather_fusion.1 = bf16[1536,2048]{1,0:T(8,128)(2,1)} fusion(bf16[1280,2048]{1,0:T(8,128)(2,1)} %bitcast.11, s32[2048]{0:T(1024)S(1)} %pad_clamp_fusion.1), kind=kCustom, calls=%fused_computation.1 | custom fusion | bytes 12589056 | tf_op jit(solution)/shard_map/gather | solution.py:97
  508.7 10.9 %reshape.230 = bf16[256,6,2048]{2,1,0:T(8,128)(2,1)} reshape(bf16[1536,2048]{1,0:T(8,128)(2,1)} %gather_fusion.1) | data formatting | bytes 12582912 | tf_op jit(solution)/shard_map/gather | solution.py:97
  519.6 7.1 %fusion.78 = f32[256,1,2048]{2,1,0:T(1,128)} fusion(bf16[256,6,2048]{2,1,0:T(8,128)(2,1)} %reshape.230, bf16[256,6,1]{1,2,0:T(2,128)(2,1)S(1)} %copy.50), kind=kOutput, calls=%fused_computation.124 | convolution fusion | flops 6291456 | bytes 8391680 | tf_op jit(solution)/shard_map/tkd,tk->td/dot_general | solution.py:98
  526.7 5.9 fusion.6
  532.6 0.0 reduce-scatter.2.cloned.1.call-update
  532.6 0.8 dynamic_slice.12
  533.4 51.3 %reduce-scatter.2.cloned.1.call-done = bf16[256,256]{1,0:T(8,128)(2,1)} async-done(((bf16[256,2048]{1,0:T(8,128)(2,1)}), bf16[256,256]{1,0:T(8,128)(2,1)}) %reduce-scatter.2.cloned.1.call-update) | async-done | bytes 131088 | tf_op jit(solution)/shard_map/reduce_scatter | solution.py:107
  584.7 1.0 fusion.47
  585.7 0.0 copy-start.2
  585.7 14.9 %psum.15 = f32[256]{0:T(256)S(1)} all-reduce(f32[256]{0:T(256)S(1)} %get-tuple-element.2), channel_id=1, replica_groups=mesh['ep'=32,'tp'=8] {'tp'}, use_global_device_ids=true, to_apply=%region_9.10 | all-reduce | flops 256 | bytes 2048 | tf_op jit(solution)/shard_map/psum | solution.py:113
  600.6 0.8 fusion.49
  (19 shorter events, 0.3 us)
Async XLA Ops:
  7.2 348.5 %copy-start = (bf16[1,352,2048]{2,1,0:T(8,128)(2,1)S(1)}, bf16[1,352,2048]{2,1,0:T(8,128)(2,1)}, u32[]{:S(2)}) copy-start(bf16[1,352,2048]{2,1,0:T(8,128)(2,1)} %param.18) | copy-start | bytes 4325380
  7.2 3.2 copy-start.4
  7.2 76.2 %all-reduce.2.cloned.1.call-start = ((), (), s32[]{:S(2)}) async-start(), calls=%async_computation.3 | async-start | bytes 4194304 | tf_op jit(solution)/shard_map/psum | solution.py:50
  83.4 2.3 copy-start.5
  106.9 241.7 %all-to-all-start = ((bf16[32,2,40,2048]{3,2,1,0:T(8,128)(2,1)}), bf16[32,2,40,2048]{3,2,1,0:T(8,128)(2,1)}, u32[]{:S(2)}, u32[]{:S(2)}) async-start(bf16[32,2,40,2048]{3,2,1,0:T(8,128)(2,1)} %broadcast_select_fusion), calls=%async_computation | async-start | bytes 20971520 | tf_op jit(solution)/shard_map/all_to_all | solution.py:75
  365.5 11.1 %copy-start.3 = (bf16[2048,64]{0,1:T(8,128)(2,1)S(1)}, bf16[2048,64]{0,1:T(8,128)(2,1)}, u32[]{:S(2)}) copy-start(bf16[2048,64]{0,1:T(8,128)(2,1)} %param.16) | copy-start | bytes 786436
  365.5 127.3 %all-to-all-start.1 = ((bf16[32,40,2048]{2,1,0:T(8,128)(2,1)}), bf16[32,40,2048]{2,1,0:T(8,128)(2,1)}, u32[]{:S(2)}, u32[]{:S(2)}) async-start(bf16[32,40,2048]{2,1,0:T(8,128)(2,1)} %convolution_convert_fusion), calls=%async_computation.1 | async-start | bytes 10485760 | tf_op jit(solution)/shard_map/all_to_all | solution.py:90
  375.7 209.0 %reduce-scatter.2.cloned.1.call-start = ((), (), s32[]{:S(2)}) async-start(), calls=%async_computation.4 | async-start | bytes 1179648 | tf_op jit(solution)/shard_map/reduce_scatter | solution.py:107
  526.7 74.7 %copy-start.1 = (bf16[1,352,2048]{2,1,0:T(8,128)(2,1)S(1)}, bf16[1,352,2048]{2,1,0:T(8,128)(2,1)}, u32[]{:S(2)}) copy-start(bf16[1,352,2048]{2,1,0:T(8,128)(2,1)} %param.18) | copy-start | bytes 4325380
  585.7 15.7 %copy-start.2 = (bf16[256,256]{1,0:T(8,128)(2,1)}, bf16[256,256]{1,0:T(8,128)(2,1)S(1)}, u32[]{:S(2)}) copy-start(bf16[256,256]{1,0:T(8,128)(2,1)S(1)} %get-tuple-element.3) | copy-start | bytes 393220
Sparse Core Ops, SparseCore 0:
  10.5 72.8 all-reduce.1
  532.7 51.9 reduce-scatter.1
where the time goes:
time: 609 us; the launch traced here: 608 us
  waiting for transfers between devices  427 us (70%)
  local copies, waits for them, and re-layouts  60.9 us (10%)
  matrix products  36.1 us (6%)
  other arithmetic  33.8 us (6%)
  starting transfers between devices  20.1 us (3%)
  between operations  15 us (2%)
  blocking collectives  14.9 us (2%)
    all_to_all x1, waiting for transfers between devices, on_device(): lax.all_to_all(dispatched, 'ep', split_axis=0, concat_axis=0, tiled=True)  232 us
    all_to_all x1, waiting for transfers between devices, on_device(): lax.all_to_all(produced, 'ep', split_axis=0, concat_axis=0, tiled=True)  99.9 us
    reduce_scatter x1, waiting for transfers between devices, on_device(): lax.psum_scatter((routed_part + shared_part).astype(jnp.bfloat16), 'tp',...  51.3 us
    psum x1, waiting for transfers between devices, on_device(): summed = lax.psum(partial_out, 'tp')  44.1 us
    gather x2, local copies, waits for them, and re-layouts, on_device(): picked = flat_terms[term_row]  26.8 us
    another operation x3, other arithmetic  18.4 us
    psum x1, blocking collectives, on_device(): squares = lax.psum(jnp.sum(next_wide * next_wide, axis=1), 'tp')  14.9 us
    gather x5, local copies, waits for them, and re-layouts, gate_weights(): chosen = jnp.take_along_axis(logits, route_block, axis=1)  13.2 us
  transfers between devices with their start and end apart: 4, of which 4 were waited for; matrix products, arithmetic and copies ran while one was open for 8% of the time, Pallas kernels for 0%

commit v1 on v0

--- a/solution.py
+++ b/solution.py
@@ -6,6 +6,11 @@
 EXP_DEV = 2
 norm_epsilon = 1e-06
 routed_scale = 2.446
+
+
+def state_the_bands(content):
+    y_new = lax.all_gather(content, axis_name="tp").sum(axis=0)
+    return y_new
 
 
 def slot_table(route_block, live_count, experts, capacity):
@@ -110,7 +115,7 @@
     stream_slice = lax.dynamic_slice_in_dim(stream, column_start, width_slice, 1)
     next_stream = (stream_slice.astype(jnp.float32) + combined).astype(jnp.bfloat16)
     next_wide = next_stream.astype(jnp.float32)
-    squares = lax.psum(jnp.sum(next_wide * next_wide, axis=1), "tp")
+    squares = state_the_bands(jnp.sum(next_wide * next_wide, axis=1))
     gain_slice = lax.dynamic_slice_in_dim(next_gain, column_start, width_slice, 0)
     next_normed = (
         next_wide * lax.rsqrt(squares[:, None] / width + norm_epsilon) * gain_slice

time: 609 us -> 605 us (level)
    psum x1 -> x0, blocking collectives: 14.9 us -> none  [on_device(): squares = lax.psum(jnp.sum(next_wide * next_wide, axis=1), 'tp')]
    all_gather x0 -> x1, blocking collectives: none -> 10.7 us  [state_the_bands(): y_new = lax.all_gather(content, axis_name='tp').sum(axis=0)]
where the time goes in v1:
time: 605 us; the launch traced here: 604 us
  waiting for transfers between devices  427 us (71%)
  local copies, waits for them, and re-layouts  60.9 us (10%)
  matrix products  36.1 us (6%)
  other arithmetic  33.9 us (6%)
  starting transfers between devices  20.1 us (3%)
  between operations  15 us (2%)
  blocking collectives  10.7 us (2%)
    all_to_all x1, waiting for transfers between devices, on_device(): lax.all_to_all(dispatched, 'ep', split_axis=0, concat_axis=0, tiled=True)  232 us
    all_to_all x1, waiting for transfers between devices, on_device(): lax.all_to_all(produced, 'ep', split_axis=0, concat_axis=0, tiled=True)  99.9 us
    reduce_scatter x1, waiting for transfers between devices, on_device(): lax.psum_scatter((routed_part + shared_part).astype(jnp.bfloat16), 'tp',...  51.3 us
    psum x1, waiting for transfers between devices, on_device(): summed = lax.psum(partial_out, 'tp')  44.1 us
    gather x2, local copies, waits for them, and re-layouts, on_device(): picked = flat_terms[term_row]  26.8 us
    another operation x3, other arithmetic  18.4 us
    gather x5, local copies, waits for them, and re-layouts, gate_weights(): chosen = jnp.take_along_axis(logits, route_block, axis=1)  13.2 us
  transfers between devices with their start and end apart: 4, of which 4 were waited for; matrix products, arithmetic and copies ran while one was open for 8% of the time, Pallas kernels for 0%

profile of v1, /device:TPU:1, one launch (start us, length us, event | category | flops | bytes accessed | tf_op | source)
XLA Modules:
  0.0 604.1 jit_solution(5712165033433359267)
XLA Ops:
  7.2 0.0 copy-start
  7.2 0.0 copy-start.4
  7.2 0.0 all-reduce.2.cloned.1.call-start
  7.2 3.1 fusion.76
  10.4 0.0 all-reduce.2.cloned.1.call-update
  10.4 0.0 copy-done.4
  10.4 0.1 copy.42
  10.5 0.1 eq.37
  10.7 0.1 eq.33
  11.5 0.1 fusion.37
  11.6 18.1 %reduce-window.6 = s32[64,12,128]{2,1,0:T(8,128)S(1)} reduce-window(s32[64,12,128]{2,1,0:T(8,128)S(1)} %fusion.37, s32[]{:T(128)} %constant.103.clone.1), window={size=1x1x128 pad=0_0x0_0x127_0}, to_apply=%region_1.0 | reduce-window | flops 12484608 | bytes 786436 | tf_op jit(solution)/shard_map/reduce-window
  29.7 0.2 slice.30
  29.9 0.3 copy.44
  30.2 0.1 copy.45
  30.3 0.2 broadcast_add_fusion
  30.5 0.2 fusion.40
  30.7 0.1 reduce_sum.52
  30.9 0.1 copy.46
  31.0 0.1 copy.41
  31.1 0.1 mul.91
  31.3 6.2 %scatter_custom_fusion = s32[2560]{0:T(1024)S(1)} fusion(s32[1536]{0:T(1024)S(1)} %fusion.67, s32[1536]{0:T(1024)S(1)} %iota.72, s32[]{:T(128)} %constant.107.clone.1), kind=kCustom, calls=%fused_computation.112 | custom fusion | bytes 10244 | tf_op jit(solution)/shard_map/scatter | solution.py:28
  37.5 0.1 ge.28
  37.7 0.7 ge.27
  38.4 0.1 div.89
  38.5 0.1 and.83
  38.6 0.1 compare_select_fusion
  38.7 0.1 reshape.227
  38.8 0.6 pad_clamp_fusion
  39.4 44.1 %all-reduce.2.cloned.1.call-done = f32[256,2048]{1,0:T(8,128)} async-done(((f32[256,2048]{1,0:T(8,128)}), f32[256,2048]{1,0:T(8,128)}) %all-reduce.2.cloned.1.call-update) | async-done | bytes 2097168 | tf_op jit(solution)/shard_map/psum | solution.py:55
  83.4 2.3 fusion.7
  85.7 0.0 copy-done.5
  85.7 0.3 fusion.9
  86.0 10.9 %gather_fusion = bf16[2560,2048]{1,0:T(8,128)(2,1)} fusion(bf16[256,2048]{1,0:T(8,128)(2,1)S(1)} %fusion.9, s32[3072]{0:T(1024)} %pad_clamp_fusion), kind=kCustom, calls=%fused_computation | custom fusion | bytes 20981760 | tf_op jit(solution)/shard_map/gather | solution.py:78
  97.0 10.0 %broadcast_select_fusion = bf16[32,2,40,2048]{3,2,1,0:T(8,128)(2,1)} fusion(bf16[32,2,40,2048]{3,2,1,0:T(8,128)(2,1)} %bitcast.84, pred[32,2,40]{2,1,0:T(4,128)(4,1)} %ge.27), kind=kLoop, calls=%fused_computation.4 | loop fusion | flops 5242880 | bytes 20974080 | tf_op jit(solution)/shard_map/jit(_where)/select_n | solution.py:78
  106.9 9.7 %all-to-all-start = ((bf16[32,2,40,2048]{3,2,1,0:T(8,128)(2,1)}), bf16[32,2,40,2048]{3,2,1,0:T(8,128)(2,1)}, u32[]{:S(2)}, u32[]{:S(2)}) async-start(bf16[32,2,40,2048]{3,2,1,0:T(8,128)(2,1)} %broadcast_select_fusion), calls=%async_computation | async-start | bytes 20971520 | tf_op jit(solution)/shard_map/all_to_all | solution.py:80
  116.6 232.0 %all-to-all-done = bf16[32,2,40,2048]{3,2,1,0:T(8,128)(2,1)} async-done(((bf16[32,2,40,2048]{3,2,1,0:T(8,128)(2,1)}), bf16[32,2,40,2048]{3,2,1,0:T(8,128)(2,1)}, u32[]{:S(2)}, u32[]{:S(2)}) %all-to-all-start) | async-done | bytes 10485792 | tf_op jit(solution)/shard_map/all_to_all | solution.py:80
  348.6 7.1 %fusion.2 = f32[32,40,352]{2,1,0:T(8,128)} fusion(bf16[32,2,40,2048]{3,2,1,0:T(8,128)(2,1)} %all-to-all-done, s32[]{:T(128)S(6)} %select_n.135, bf16[1,2,352,2048]{3,2,1,0:T(8,128)(2,1)} %param.17), kind=kOutput, calls=%fused_computation.7 | convolution fusion | flops 1845493760 | bytes 8486916 | tf_op jit(solution)/shard_map/scd,fd->scf/dot_general | solution.py:85
  355.7 0.0 copy-done
  355.7 9.8 %convolution_convert_fusion = bf16[32,40,2048]{2,1,0:T(8,128)(2,1)} fusion(bf16[1,352,2048]{2,1,0:T(8,128)(2,1)S(1)} %copy-done, f32[32,40,352]{2,1,0:T(8,128)} %fusion.2, bf16[32,2,40,2048]{3,2,1,0:T(8,128)(2,1)} %all-to-all-done, s32[]{:T(128)S(6)} %select_n.135, bf16[1,2,352,2048]{3,2,1,0:T(8,128)(2,1)} %param.17), kind=kOutput, calls=%fused_computation.11 | convolution fusion | flops 3696312320 | bytes 15335428 | tf_op jit(solution)/shard_map/scf,fd->scd/dot_general | solution.py:92
  365.5 10.2 %all-to-all-start.1 = ((bf16[32,40,2048]{2,1,0:T(8,128)(2,1)}), bf16[32,40,2048]{2,1,0:T(8,128)(2,1)}, u32[]{:S(2)}, u32[]{:S(2)}) async-start(bf16[32,40,2048]{2,1,0:T(8,128)(2,1)} %convolution_convert_fusion), calls=%async_computation.1 | async-start | bytes 10485760 | tf_op jit(solution)/shard_map/all_to_all | solution.py:95
  375.7 0.2 reduce-scatter.2.cloned.1.call-start
  375.9 0.1 copy.47
  376.1 0.1 reshape.235
  376.2 0.1 copy.48
  376.4 0.1 reshape.241
  376.6 0.0 copy-done.3
  376.6 0.4 fusion.77
  377.0 12.7 %gather_fusion.2 = f32[1536]{0:T(1024)S(1)} fusion(f32[256,64]{0,1:T(8,128)S(1)} %fusion.77, s32[1536]{0:T(1024)S(1)} %reshape.241), kind=kCustom, calls=%fused_computation.2 | custom fusion | bytes 24576 | tf_op jit(solution)/shard_map/jit(take_along_axis)/gather | solution.py:35
  389.7 0.1 reshape.244
  389.9 0.1 copy.49
  390.0 0.2 copy.50
  390.2 2.7 fusion.16
  392.9 99.9 %all-to-all-done.1 = bf16[32,40,2048]{2,1,0:T(8,128)(2,1)} async-done(((bf16[32,40,2048]{2,1,0:T(8,128)(2,1)}), bf16[32,40,2048]{2,1,0:T(8,128)(2,1)}, u32[]{:S(2)}, u32[]{:S(2)}) %all-to-all-start.1) | async-done | bytes 5242912 | tf_op jit(solution)/shard_map/all_to_all | solution.py:95
  492.8 15.8 %gather_fusion.1 = bf16[1536,2048]{1,0:T(8,128)(2,1)} fusion(bf16[1280,2048]{1,0:T(8,128)(2,1)} %bitcast.11, s32[2048]{0:T(1024)S(1)} %pad_clamp_fusion.1), kind=kCustom, calls=%fused_computation.1 | custom fusion | bytes 12589056 | tf_op jit(solution)/shard_map/gather | solution.py:102
  508.7 10.9 %reshape.234 = bf16[256,6,2048]{2,1,0:T(8,128)(2,1)} reshape(bf16[1536,2048]{1,0:T(8,128)(2,1)} %gather_fusion.1) | data formatting | bytes 12582912 | tf_op jit(solution)/shard_map/gather | solution.py:102
  519.6 7.1 %fusion.78 = f32[256,1,2048]{2,1,0:T(1,128)} fusion(bf16[256,6,2048]{2,1,0:T(8,128)(2,1)} %reshape.234, bf16[256,6,1]{1,2,0:T(2,128)(2,1)S(1)} %copy.50), kind=kOutput, calls=%fused_computation.124 | convolution fusion | flops 6291456 | bytes 8391680 | tf_op jit(solution)/shard_map/tkd,tk->td/dot_general | solution.py:103
  526.7 5.9 fusion.6
  532.6 0.0 reduce-scatter.2.cloned.1.call-update
  532.6 0.8 dynamic_slice.12
  533.4 51.3 %reduce-scatter.2.cloned.1.call-done = bf16[256,256]{1,0:T(8,128)(2,1)} async-done(((bf16[256,2048]{1,0:T(8,128)(2,1)}), bf16[256,256]{1,0:T(8,128)(2,1)}) %reduce-scatter.2.cloned.1.call-update) | async-done | bytes 131088 | tf_op jit(solution)/shard_map/reduce_scatter | solution.py:112
  584.7 1.0 fusion.47
  585.7 0.0 copy-start.2
  585.7 10.7 %all-gather.1 = f32[8,1,256]{2,1,0:T(1,128)S(1)} all-gather(f32[1,1,256]{2,1,0:T(1,128)S(1)} %bitcast.88), channel_id=2, replica_groups=mesh['ep'=32,'tp'=8] {'tp'}, dimensions={0}, use_global_device_ids=true | all-gather | bytes 9216 | tf_op jit(solution)/shard_map/all_gather | solution.py:12
  596.5 0.8 fusion.49
  (20 shorter events, 0.3 us)
Async XLA Ops:
  7.2 348.5 %copy-start = (bf16[1,352,2048]{2,1,0:T(8,128)(2,1)S(1)}, bf16[1,352,2048]{2,1,0:T(8,128)(2,1)}, u32[]{:S(2)}) copy-start(bf16[1,352,2048]{2,1,0:T(8,128)(2,1)} %param.18) | copy-start | bytes 4325380
  7.2 3.2 copy-start.4
  7.2 76.2 %all-reduce.2.cloned.1.call-start = ((), (), s32[]{:S(2)}) async-start(), calls=%async_computation.3 | async-start | bytes 4194304 | tf_op jit(solution)/shard_map/psum | solution.py:55
  83.4 2.3 copy-start.5
  106.9 241.7 %all-to-all-start = ((bf16[32,2,40,2048]{3,2,1,0:T(8,128)(2,1)}), bf16[32,2,40,2048]{3,2,1,0:T(8,128)(2,1)}, u32[]{:S(2)}, u32[]{:S(2)}) async-start(bf16[32,2,40,2048]{3,2,1,0:T(8,128)(2,1)} %broadcast_select_fusion), calls=%async_computation | async-start | bytes 20971520 | tf_op jit(solution)/shard_map/all_to_all | solution.py:80
  365.5 11.1 %copy-start.3 = (bf16[2048,64]{0,1:T(8,128)(2,1)S(1)}, bf16[2048,64]{0,1:T(8,128)(2,1)}, u32[]{:S(2)}) copy-start(bf16[2048,64]{0,1:T(8,128)(2,1)} %param.16) | copy-start | bytes 786436
  365.5 127.3 %all-to-all-start.1 = ((bf16[32,40,2048]{2,1,0:T(8,128)(2,1)}), bf16[32,40,2048]{2,1,0:T(8,128)(2,1)}, u32[]{:S(2)}, u32[]{:S(2)}) async-start(bf16[32,40,2048]{2,1,0:T(8,128)(2,1)} %convolution_convert_fusion), calls=%async_computation.1 | async-start | bytes 10485760 | tf_op jit(solution)/shard_map/all_to_all | solution.py:95
  375.7 209.0 %reduce-scatter.2.cloned.1.call-start = ((), (), s32[]{:S(2)}) async-start(), calls=%async_computation.4 | async-start | bytes 1179648 | tf_op jit(solution)/shard_map/reduce_scatter | solution.py:112
  526.7 70.6 %copy-start.1 = (bf16[1,352,2048]{2,1,0:T(8,128)(2,1)S(1)}, bf16[1,352,2048]{2,1,0:T(8,128)(2,1)}, u32[]{:S(2)}) copy-start(bf16[1,352,2048]{2,1,0:T(8,128)(2,1)} %param.18) | copy-start | bytes 4325380
  585.7 11.6 %copy-start.2 = (bf16[256,256]{1,0:T(8,128)(2,1)}, bf16[256,256]{1,0:T(8,128)(2,1)S(1)}, u32[]{:S(2)}) copy-start(bf16[256,256]{1,0:T(8,128)(2,1)S(1)} %get-tuple-element.3) | copy-start | bytes 393220
Sparse Core Ops, SparseCore 0:
  10.5 72.8 all-reduce.1
  532.7 51.9 reduce-scatter.1
